TPU v7x, 32 devices: a whole 2x2x4 slice. The times are simulated.
32 devices in a mesh: dp: 8 (over z, y), mp: 4 (over x, core).
Axes of the slice: x: 2, y: 2, z: 4, core: 2. Of those that a mesh axis runs over, the one named last changes fastest.
Arguments:
- hidden_in: bfloat16 [32768, 768], P(('dp', 'mp')), may hold values from -37 to 37
- out_grad: bfloat16 [32768, 768], P(('dp', 'mp')), may hold values from -18 to 18
- seq_len: int32 [8], P('dp'), may hold values from 1024 to 4096, as said below
- owner_list: int32 [24], replicated, may hold values from 0 to 7, as said below
- block_master: float32 [4, 8, 768, 194], P('mp', 'dp'), may hold values from -0.4690971 to 0.4690971
- block_first: float32 [4, 8, 768, 194], P('mp', 'dp'), may hold values from -2048 to 2048
- block_second: float32 [4, 8, 768, 194], P('mp', 'dp'), may hold values from 131072 to 524288
- block_ema: float32 [4, 8, 768, 194], P('mp', 'dp'), may hold values from -0.21875 to 0.21875
- head_small: float32 [24, 10, 64], P('mp'), may hold values from -10 to 3
- head_first: float32 [24, 10, 64], P('mp'), may hold values from -1024 to 1024
- head_second: float32 [24, 10, 64], P('mp'), may hold values from 32768 to 131072
- head_ema: float32 [24, 10, 64], P('mp'), may hold values from -6 to 6
- bc_weight: float32 [768, 256], replicated, may hold values from -0.21875 to 0.21875
- bc_first: float32 [768, 256], replicated, may hold values from -1024 to 1024
- bc_second: float32 [768, 256], replicated, may hold values from 32768 to 131072
- bc_ema: float32 [768, 256], replicated, may hold values from -0.21875 to 0.21875
- shared_small: float32 [10, 256], replicated, may hold values from 0.25 to 1.25
- shared_first: float32 [10, 256], replicated, may hold values from -1024 to 1024
- shared_second: float32 [10, 256], replicated, may hold values from 32768 to 131072
- shared_ema: float32 [10, 256], replicated, may hold values from 0.25 to 1.25
Outputs:
- hidden_out: bfloat16 [32768, 768], P(('dp', 'mp'))
- hidden_grad: float32 [32768, 768], P(('dp', 'mp'))
- block_master_new: float32 [4, 8, 768, 194], P('mp', 'dp')
- block_first_new: float32 [4, 8, 768, 194], P('mp', 'dp')
- block_second_new: float32 [4, 8, 768, 194], P('mp', 'dp')
- block_ema_new: float32 [4, 8, 768, 194], P('mp', 'dp')
- head_small_new: float32 [24, 10, 64], P('mp')
- head_first_new: float32 [24, 10, 64], P('mp')
- head_second_new: float32 [24, 10, 64], P('mp')
- head_ema_new: float32 [24, 10, 64], P('mp')
- bc_weight_new: float32 [768, 256], replicated
- bc_first_new: float32 [768, 256], replicated
- bc_second_new: float32 [768, 256], replicated
- bc_ema_new: float32 [768, 256], replicated
- shared_small_new: float32 [10, 256], replicated
- shared_first_new: float32 [10, 256], replicated
- shared_second_new: float32 [10, 256], replicated
- shared_ema_new: float32 [10, 256], replicated
Inputs may be any that keep to these rules, and one draw needn't show every extreme that they name: `seq_len`: all sequences of a group have the same length, one of 1024, 2048, 4096; each of the three occurs in every draw. `owner_list`: the 6 heads of one index of mp (heads i * 6 to (i + 1) * 6 - 1) have distinct owners.
All inputs are finite; a program needn't handle non-finite values.
Results may differ from a plain program's by a relative error of at most 0.01.
Values may be sent and summed in bfloat16 or wider, within the bound.
No kernel may reach another device: no remote copies, remote signals or barrier semaphores. Data moves between devices by JAX's collectives and lax.ppermute only.
A program may use at most 448 MiB of HBM per device.

v0:
```python
import jax
import jax.numpy as jnp
from jax import lax
from jax.sharding import PartitionSpec as P

D = 768
H = 24
P_SIZE = 64
K = 7
BLOCK_LEN = 256
STEP = 3
PRECISE = lax.Precision.HIGHEST
NORM_EPS = 1e-05
BETA_ONE = 0.5
BETA_TWO = 0.5
ADAM_EPS = 1e-08
WEIGHT_DECAY = 0.1
MATRIX_RATE = 0.04
SMALL_RATE = 0.2
AVERAGE_KEEP = 0.75


def conv_centered(signal, filter_taps, seq_length):
    row_count = signal.shape[0]
    tap_count = filter_taps.shape[0]
    half_taps = tap_count // 2
    position = jnp.arange(row_count, dtype=jnp.int32) % seq_length
    padded = jnp.pad(signal, ((half_taps, half_taps), (0, 0)))
    summed = jnp.zeros_like(signal)
    for tap_index in range(tap_count):
        offset = tap_index - half_taps
        shifted = padded[tap_index : tap_index + row_count]
        inside = (position + offset >= 0) & (position + offset < seq_length)
        summed = summed + jnp.where(inside[:, None], shifted, 0.0) * filter_taps[tap_index][None, :]
    return summed


def shift_down(values, seq_length):
    shifted = jnp.concatenate([jnp.zeros_like(values[:1]), values[:-1]], axis=0)
    position = jnp.arange(values.shape[0], dtype=jnp.int32) % seq_length
    return jnp.where((position > 0)[:, None, None], shifted, 0.0)


def within_blocks(values_blk, b_blk, c_blk, rates_blk):
    log_decay = jnp.transpose(jnp.cumsum(-rates_blk, axis=1), (0, 2, 1))
    block_size = rates_blk.shape[1]
    scores = jnp.einsum("bin,bjn->bij", c_blk, b_blk, precision=PRECISE)
    causal_mask = (jnp.arange(block_size)[:, None] >= jnp.arange(block_size)[None, :])[None, None]
    log_gap = log_decay[:, :, :, None] - log_decay[:, :, None, :]
    decay_mat = jnp.where(causal_mask, jnp.exp(jnp.where(causal_mask, log_gap, -60.0)), 0.0)
    weights = decay_mat * scores[:, None] * jnp.transpose(rates_blk, (0, 2, 1))[:, :, None, :]
    inner_part = jnp.einsum("bhij,bjhp->bihp", weights, values_blk, precision=PRECISE)
    tail_decay = jnp.exp(log_decay[:, :, -1:] - log_decay) * jnp.transpose(rates_blk, (0, 2, 1))
    local_state = jnp.einsum("bjn,bhj,bjhp->bhnp", b_blk, tail_decay, values_blk, precision=PRECISE)
    return (inner_part, local_state, log_decay)


def carry_state(state_in, pieces):
    local_state, total_decay, keep_flag = pieces
    entering = state_in * keep_flag
    new_state = entering * jnp.exp(total_decay)[:, None, None] + local_state
    return (new_state, entering)


def state_mix(values, b_vectors, c_vectors, step_rates, seq_length):
    row_count, head_count, head_width = values.shape
    blocks = row_count // BLOCK_LEN
    keep_flags = (jnp.arange(blocks, dtype=jnp.int32) * BLOCK_LEN % seq_length != 0).astype(
        jnp.float32
    )
    values_blk = values.reshape(blocks, BLOCK_LEN, head_count, head_width)
    b_blk = b_vectors.reshape(blocks, BLOCK_LEN, -1)
    c_blk = c_vectors.reshape(blocks, BLOCK_LEN, -1)
    rates_blk = step_rates.reshape(blocks, BLOCK_LEN, head_count)
    inner_part, local_state, log_decay = jax.checkpoint(within_blocks)(
        values_blk, b_blk, c_blk, rates_blk
    )
    initial = jnp.zeros((head_count, b_vectors.shape[1], head_width), jnp.float32)
    _, entering_all = lax.scan(carry_state, initial, (local_state, log_decay[:, :, -1], keep_flags))
    cross_part = jnp.einsum("bin,bhnp->bihp", c_blk, entering_all, precision=PRECISE)
    cross_part = cross_part * jnp.transpose(jnp.exp(log_decay), (0, 2, 1))[:, :, :, None]
    return (inner_part + cross_part).reshape(row_count, head_count, head_width)


def local_mix(proj_heads, proj_keys, head_params, key_taps, seq_length):
    row_count, head_count, _ = proj_heads.shape
    head_width = head_params.shape[2]
    tap_count = key_taps.shape[0]
    gate_part = proj_heads[:, :, :head_width]
    value_part = proj_heads[:, :, head_width : 2 * head_width].reshape(
        row_count, head_count * head_width
    )
    rate_part = proj_heads[:, :, 2 * head_width : 2 * head_width + 2]
    value_taps = jnp.transpose(head_params[:, 1 : 1 + tap_count, :], (1, 0, 2)).reshape(
        tap_count, head_count * head_width
    )
    values = jax.nn.silu(conv_centered(value_part, value_taps, seq_length)).reshape(
        row_count, head_count, head_width
    )
    key_signal = jax.nn.silu(conv_centered(proj_keys, key_taps, seq_length))
    state_size = key_signal.shape[1] // 4
    forward_b = key_signal[:, :state_size]
    forward_c = key_signal[:, state_size : 2 * state_size]
    reverse_b = key_signal[:, 2 * state_size : 3 * state_size]
    reverse_c = key_signal[:, 3 * state_size :]
    step_rates = jax.nn.softplus(rate_part + head_params[None, :, tap_count + 2, :2])
    diagonal = head_params[:, tap_count + 1, :]
    forward = shift_down(
        state_mix(values, forward_b, forward_c, step_rates[:, :, 0], seq_length), seq_length
    )
    backward = shift_down(
        state_mix(
            values[::-1], reverse_b[::-1], reverse_c[::-1], step_rates[::-1, :, 1], seq_length
        ),
        seq_length,
    )[::-1]
    mixture = forward + backward + values * diagonal[None]
    return mixture * jax.nn.silu(gate_part)


def adamw_update(weight, gradient, first_moment, second, average, step_rate):
    first_new = BETA_ONE * first_moment + (1.0 - BETA_ONE) * gradient
    second_new = BETA_TWO * second + (1.0 - BETA_TWO) * gradient * gradient
    correct_one = 1.0 - BETA_ONE**STEP
    correct_two = 1.0 - BETA_TWO**STEP
    normalized = first_new / correct_one / (jnp.sqrt(second_new / correct_two) + ADAM_EPS)
    weight_new = weight - step_rate * (normalized + WEIGHT_DECAY * weight)
    average_new = AVERAGE_KEEP * average + (1.0 - AVERAGE_KEEP) * weight_new
    return (weight_new, first_new, second_new, average_new)


def local(
    hidden_in,
    out_grad,
    seq_len,
    owner_list,
    block_master,
    block_first,
    block_second,
    block_ema,
    head_small,
    head_first,
    head_second,
    head_ema,
    bc_weight,
    bc_first,
    bc_second,
    bc_ema,
    shared_small,
    shared_first,
    shared_second,
    shared_ema,
):
    heads_here = head_small.shape[0]
    mp_index = lax.axis_index("mp")
    dp_index = lax.axis_index("dp")
    seq_length = seq_len[0]
    owners_here = lax.dynamic_slice_in_dim(owner_list, mp_index * heads_here, heads_here)
    slot_low = block_master[0].astype(jnp.bfloat16)
    all_slots = lax.all_gather(slot_low, "dp", axis=0, tiled=True)
    blocks = jnp.take(all_slots, owners_here, axis=0)
    in_width = 2 * P_SIZE + 2
    w_in_flat = jnp.transpose(blocks[:, :, :in_width], (1, 0, 2)).reshape(D, heads_here * in_width)
    w_out_flat = jnp.transpose(blocks[:, :, in_width:], (0, 2, 1)).reshape(heads_here * P_SIZE, D)
    key_low = bc_weight.astype(jnp.bfloat16)
    key_taps = shared_small[:K]
    gain_in = shared_small[K:].reshape(D)
    hidden = hidden_in.astype(jnp.float32)
    scale_in = lax.rsqrt(jnp.mean(hidden * hidden, axis=1, keepdims=True) + NORM_EPS)
    normed_low = (hidden * scale_in * gain_in).astype(jnp.bfloat16)
    features = lax.all_gather(normed_low, "mp", axis=0, tiled=True)
    group_rows = features.shape[0]
    proj_heads = jnp.dot(features, w_in_flat, preferred_element_type=jnp.float32).reshape(
        group_rows, heads_here, in_width
    )
    proj_keys = jnp.dot(features, key_low, preferred_element_type=jnp.float32)

    def mixing(heads_in, keys_in, params_in, taps_in):
        return local_mix(heads_in, keys_in, params_in, taps_in, seq_length)

    gated_mix, mix_pullback = jax.vjp(mixing, proj_heads, proj_keys, head_small, key_taps)
    gain_mix = head_small[:, 0, :]
    square_rows = jnp.sum(gated_mix * gated_mix, axis=(1, 2))
    square_total = lax.psum(square_rows, "mp")
    scale_mix = lax.rsqrt(square_total / (H * P_SIZE) + NORM_EPS)[:, None, None]
    normal_mix = gated_mix * scale_mix
    result_low = (
        (normal_mix * gain_mix[None]).astype(jnp.bfloat16).reshape(group_rows, heads_here * P_SIZE)
    )
    rows_in = result_low
    branch_out = lax.psum_scatter(
        jnp.dot(rows_in, w_out_flat, preferred_element_type=jnp.float32),
        "mp",
        scatter_dimension=0,
        tiled=True,
    )
    hidden_out = (hidden + branch_out).astype(jnp.bfloat16)
    grad_full = lax.all_gather(out_grad, "mp", axis=0, tiled=True)
    out_weight_grad = lax.dot_general(
        result_low, grad_full, (((0,), (0,)), ((), ())), preferred_element_type=jnp.float32
    )
    result_grad = lax.dot_general(
        grad_full, w_out_flat, (((1,), (1,)), ((), ())), preferred_element_type=jnp.float32
    ).reshape(group_rows, heads_here, P_SIZE)
    gain_mix_grad = jnp.sum(result_grad * normal_mix, axis=0)
    normal_grad = result_grad * gain_mix[None]
    cross_rows = jnp.sum(normal_grad * gated_mix, axis=(1, 2))
    cross_total = lax.psum(cross_rows, "mp")
    gated_grad = (
        scale_mix * normal_grad
        - gated_mix * scale_mix**3 * (cross_total / (H * P_SIZE))[:, None, None]
    )
    heads_grad, keys_grad, params_grad, taps_grad = mix_pullback(gated_grad)
    params_grad = params_grad.at[:, 0, :].add(gain_mix_grad)
    heads_low = heads_grad.reshape(group_rows, heads_here * in_width).astype(jnp.bfloat16)
    keys_own = lax.psum_scatter(keys_grad, "mp", scatter_dimension=0, tiled=True)
    keys_low = keys_own.astype(jnp.bfloat16)
    in_weight_grad = lax.dot_general(
        features, heads_low, (((0,), (0,)), ((), ())), preferred_element_type=jnp.float32
    )
    in_weight_grad = jnp.transpose(in_weight_grad.reshape(D, heads_here, in_width), (1, 0, 2))
    block_grad = jnp.concatenate(
        [in_weight_grad, jnp.transpose(out_weight_grad.reshape(heads_here, P_SIZE, D), (0, 2, 1))],
        axis=2,
    )
    key_weight_grad = lax.dot_general(
        normed_low, keys_low, (((0,), (0,)), ((), ())), preferred_element_type=jnp.float32
    )
    rows_in = heads_low
    normed_grad = lax.psum_scatter(
        lax.dot_general(
            rows_in, w_in_flat, (((1,), (1,)), ((), ())), preferred_element_type=jnp.float32
        ),
        "mp",
        scatter_dimension=0,
        tiled=True,
    )
    normed_grad = normed_grad + lax.dot_general(
        keys_low, key_low, (((1,), (1,)), ((), ())), preferred_element_type=jnp.float32
    )
    gain_in_grad = jnp.sum(normed_grad * hidden * scale_in, axis=0)
    scaled_in = normed_grad * gain_in
    cross_in = jnp.sum(scaled_in * hidden, axis=1, keepdims=True)
    hidden_grad = (
        out_grad.astype(jnp.float32) + scale_in * scaled_in - hidden * scale_in**3 * cross_in / D
    )
    shared_grad = jnp.concatenate([taps_grad, gain_in_grad.reshape(-1, taps_grad.shape[1])], axis=0)
    block_total, params_total = lax.psum((block_grad, params_grad), "dp")
    key_total, shared_total = lax.psum((key_weight_grad, shared_grad), ("dp", "mp"))
    head_new = adamw_update(head_small, params_total, head_first, head_second, head_ema, SMALL_RATE)
    key_new = adamw_update(bc_weight, key_total, bc_first, bc_second, bc_ema, MATRIX_RATE)
    shared_new = adamw_update(
        shared_small, shared_total, shared_first, shared_second, shared_ema, SMALL_RATE
    )
    owned_mask = (owners_here == dp_index).astype(jnp.float32)
    own_grad = jnp.tensordot(owned_mask, block_total, axes=1)
    is_owner = jnp.sum(owned_mask) > 0.5
    previous_all = (block_master[0, 0], block_first[0, 0], block_second[0, 0], block_ema[0, 0])
    slot_new = adamw_update(
        previous_all[0], own_grad, previous_all[1], previous_all[2], previous_all[3], MATRIX_RATE
    )
    slot_outs = [
        jnp.where(is_owner, renewed, previous)[None, None]
        for renewed, previous in zip(slot_new, previous_all)
    ]
    return (
        hidden_out,
        hidden_grad,
        slot_outs[0],
        slot_outs[1],
        slot_outs[2],
        slot_outs[3],
        head_new[0],
        head_new[1],
        head_new[2],
        head_new[3],
        key_new[0],
        key_new[1],
        key_new[2],
        key_new[3],
        shared_new[0],
        shared_new[1],
        shared_new[2],
        shared_new[3],
    )


def solution(mesh):
    placed = (
        P(("dp", "mp"), None),
        P(("dp", "mp"), None),
        P("dp"),
        P(),
        P("mp", "dp", None, None),
        P("mp", "dp", None, None),
        P("mp", "dp", None, None),
        P("mp", "dp", None, None),
        P("mp", None, None),
        P("mp", None, None),
        P("mp", None, None),
        P("mp", None, None),
        P(),
        P(),
        P(),
        P(),
        P(),
        P(),
        P(),
        P(),
    )
    return jax.shard_map(
        local,
        mesh=mesh,
        in_specs=placed,
        out_specs=(
            P(("dp", "mp"), None),
            P(("dp", "mp"), None),
            P("mp", "dp", None, None),
            P("mp", "dp", None, None),
            P("mp", "dp", None, None),
            P("mp", "dp", None, None),
            P("mp", None, None),
            P("mp", None, None),
            P("mp", None, None),
            P("mp", None, None),
            P(),
            P(),
            P(),
            P(),
            P(),
            P(),
            P(),
            P(),
        ),
        check_vma=False,
    )
```

profile of v0, /device:TPU:0, one launch (start us, length us, event | category | flops | bytes accessed | tf_op | source)
XLA Modules:
  0.0 1658.8 jit_solution(6648036908415490787)
XLA Ops:
  21.4 45.3 %all-gather.9.cloned.1.call-done = bf16[8,1,768,194]{2,3,1,0:T(8,128)(2,1)} async-done(((bf16[1,1,768,194]{2,3,1,0:T(8,128)(2,1)}), bf16[8,1,768,194]{2,3,1,0:T(8,128)(2,1)}) %all-gather.9.cloned.1.call-update) | async-done | bytes 2383888 | tf_op jit(solution)/shard_map/all_gather | solution.py:160
  74.7 39.1 %all-gather.5.cloned.1.call-done = bf16[4096,768]{1,0:T(8,128)(2,1)} async-done(((bf16[1024,768]{1,0:T(8,128)(2,1)}), bf16[4096,768]{1,0:T(8,128)(2,1)}) %all-gather.5.cloned.1.call-update) | async-done | bytes 6291472 | tf_op jit(solution)/shard_map/all_gather | solution.py:171
  132.1 13.7 rev.33
  173.2 29.2 %fusion.98 = (f32[4096,384]{0,1:T(8,128)}, f32[4096,384]{0,1:T(8,128)}) fusion(f32[384]{0:T(512)S(1)} %mul.996, pred[4096]{0:T(1024)(128)(4,1)S(1)} %get-tuple-element.1093, f32[384]{0:T(512)S(1)} %mul.993, pred[4096]{0:T(1024)(128)(4,1)S(1)} %get-tuple-element.1094, f32[384]{0:T(512)S(1)} %mul.990, pred[4096]{0:T(1024)(128)(4,1)S(1)} %get-tuple-element.1095, ...), kind=kLoop, calls=%fused_computation.187 | loop fusion | flops 37748736 | bytes 18913792 | tf_op jit(solution)/shard_map/jvp(jit(silu))/mul | solution.py:97
  202.5 20.0 %rev.30 = f32[4096,6,64]{0,2,1:T(8,128)} reverse(f32[4096,6,64]{0,2,1:T(8,128)} %bitcast.605), dimensions={0} | reverse | bytes 12582912 | tf_op jit(solution)/shard_map/jvp()/rev | solution.py:113
  233.5 60.7 %while.74 = (s32[]{:T(128)}, f32[6,64,64]{2,1,0:T(8,128)S(1)}, f32[16,6,64,64]{3,2,1,0:T(8,128)}, f32[16,6]{1,0:T(8,128)S(1)}, f32[16,6,1,1]{1,3,2,0:T(1,128)S(1...) while((s32[]{:T(128)}, f32[6,64,64]{2,1,0:T(8,128)S(1)}, ...), condition=%wide.region_8.9_spmd.clone, body=%wide.region_7.8_spmd.clone.sunk | while | flops 147459 | bytes 985312 | solution.py:79
  316.3 60.5 %while.73 = (s32[]{:T(128)}, f32[6,64,64]{2,1,0:T(8,128)S(1)}, f32[16,6,64,64]{3,2,1,0:T(8,128)}, f32[16,6]{1,0:T(8,128)S(1)}, f32[16,6,1,1]{1,3,2,0:T(1,128)S(1...) while((s32[]{:T(128)}, f32[6,64,64]{2,1,0:T(8,128)S(1)}, ...), condition=%wide.region_4.5_spmd.clone, body=%wide.region_3.4_spmd.clone.sunk | while | flops 147459 | bytes 985312 | solution.py:79
  376.9 16.5 rev.32
  411.2 29.6 %fusion.84 = f32[16,6,8,8,256]{4,3,2,1,0:T(8,128)S(1)} fusion(f32[16,256,6,64]{1,3,2,0:T(8,128)S(1)} %bitcast.666, f32[16,256,6]{1,2,0:T(8,128)S(1)} %get-tuple-element.1065, f32[16,6,256]{2,1,0:T(8,128)S(1)} %copy.611, f32[16,256,256]{2,1,0:T(8,128)S(1)} %fusion.278, f32[16,6,256]{2,1,0:T(8,128)S(1)} %get-tuple-element.1064, ...), kind=kOutput, calls=%fused_computation.144 | convolution fusion | flops 4866441216 | bytes 23429120 | tf_op jit(solution)/shard_map/jvp(bhij,bjhp->bihp)/dot_general | solution.py:52
  446.0 20.1 %rev.34 = f32[4096,6,64]{0,2,1:T(8,128)} reverse(f32[4096,6,64]{0,2,1:T(8,128)} %pad_select_fusion), dimensions={0} | reverse | bytes 12582912 | tf_op jit(solution)/shard_map/jvp()/rev | solution.py:111
  484.8 34.4 %fusion.85 = f32[16,6,8,8,256]{4,3,2,1,0:T(8,128)} fusion(f32[16,256,6,64]{1,3,2,0:T(8,128)} %bitcast.668, f32[16,256,6]{1,2,0:T(8,128)S(1)} %get-tuple-element.1063, f32[16,6,256]{2,1,0:T(8,128)S(1)} %copy.593, f32[16,256,256]{2,1,0:T(8,128)} %fusion.276, f32[16,6,256]{2,1,0:T(8,128)S(1)} %get-tuple-element.1062, pred[256,256]{1,0:T(8,128)(4,1)S(1)} %copy-done.79, ...), kind=kOutput, calls=%fused_computation.146 | convolution fusion | flops 4866441216 | bytes 23429120 | tf_op jit(solution)/shard_map/jvp(bhij,bjhp->bihp)/dot_general | solution.py:52
  562.7 17.4 %multiply_reduce_fusion.14 = (f32[6,64]{1,0:T(8,128)}, f32[4096,6,64]{0,2,1:T(8,128)}, f32[4096,6,64]{0,2,1:T(8,128)}) fusion(f32[4096,6,64]{0,2,1:T(8,128)} %bitcast.607, f32[4096,6,130]{0,2,1:T(8,128)} %copy-done.20, f32[4096]{0:T(1024)S(1)} %broadcast_multiply_fusion.1, f32[4096,6,64]{0,2,1:T(8,128)} %get-tuple-element.1013, ...), kind=kLoop, calls=%fused_computation.164 | loop fusion | flops 29884032 | bytes 44092416 | tf_op jit(solution)/shard_map/transpose(jvp())/reduce_sum | solution.py:117
  580.1 20.4 %rev.35 = f32[4096,6,64]{0,2,1:T(8,128)} reverse(f32[4096,6,64]{0,2,1:T(8,128)} %get-tuple-element.1008), dimensions={0} | reverse | bytes 12582912 | tf_op jit(solution)/shard_map/transpose(jvp())/rev | solution.py:111
  600.6 12.5 slice_select_fusion.1
  649.1 76.9 %while.76 = (s32[]{:T(128)}, f32[6,64,64]{2,1,0:T(8,128)S(1)}, f32[16,6,64,64]{3,2,1,0:T(8,128)}, f32[16,6]{1,0:T(8,128)S(1)}, f32[16,6,64,64]{2,3,1,0:T(8,128)}...) while((s32[]{:T(128)}, f32[6,64,64]{2,1,0:T(8,128)S(1)}, ...), condition=%wide.region_28.29_spmd.clone, body=%wide.region_26.28_spmd.clone.sunk | while | flops 172036 | bytes 1081748 | solution.py:79
  754.8 87.2 %while.75 = (s32[]{:T(128)}, f32[6,64,64]{2,1,0:T(8,128)S(1)}, f32[16,6,64,64]{3,2,1,0:T(8,128)}, f32[16,6]{1,0:T(8,128)S(1)}, f32[16,6,64,64]{2,3,1,0:T(8,128)}...) while((s32[]{:T(128)}, f32[6,64,64]{2,1,0:T(8,128)S(1)}, ...), condition=%wide.region_16.17_spmd.clone, body=%wide.region_14.16_spmd.clone.sunk | while | flops 172036 | bytes 1081748 | solution.py:79
  900.3 35.2 %fusion.79 = f32[16,6,256,256]{3,2,1,0:T(8,128)} fusion(f32[16,256,6,64]{1,0,3,2:T(8,128)} %bitcast.598, f32[16,256,6,64]{1,0,3,2:T(8,128)} %bitcast.655), kind=kOutput, calls=%fused_computation.138 | convolution fusion | flops 4831838208 | bytes 37748736 | tf_op jit(solution)/shard_map/transpose(jvp(jvp()))/checkpoint/bhij,bjhp->bihp/dot_general | solution.py:52
  935.6 66.6 %fusion.35 = (f32[16,6,256]{2,1,0:T(8,128)}, f32[16,6,256]{2,1,0:T(8,128)}, f32[16,6,256]{2,1,0:T(8,128)}, f32[16,256,256]{2,1,0:T(8,128)}, f32[16,256,256]{2,1,...) fusion(f32[16,6,256]{2,1,0:T(8,128)S(1)} %bitcast.704, ...), kind=kOutput, calls=%fused_computation.67 | convolution fusion | flops 5018337280 | bytes 55574528 | tf_op jit(solution)/shard_map/transpose(jvp(jvp()))/checkpoint/bhij,bjhp->bihp/dot_general | solution.py:52
  1012.5 26.9 %fusion.76 = f32[16,6,8,8,256]{4,3,2,1,0:T(8,128)} fusion(f32[16,256,6,64]{1,3,2,0:T(8,128)S(1)} %copy-done.38, f32[16,256,6]{1,2,0:T(8,128)S(1)} %get-tuple-element.1055, f32[16,6,256]{2,1,0:T(8,128)S(1)} %bitcast.703, f32[16,256,256]{2,1,0:T(8,128)} %fusion.282, f32[16,6,256]{2,1,0:T(8,128)S(1)} %copy-done.76, pred[256,256]{1,0:T(8,128)(4,1)S(1)} %copy-done.80, ...), kind=kOutput, calls=%fused_computation.134 | convolution fusion | flops 4866441216 | bytes 23429120 | tf_op jit(solution)/shard_map/transpose(jvp(jvp()))/checkpoint/bhij,bjhp->bihp/dot_general | solution.py:52
  1067.0 26.3 %fusion.77 = f32[16,6,8,8,256]{4,3,2,1,0:T(8,128)} fusion(f32[16,256,6,64]{1,3,2,0:T(8,128)S(1)} %bitcast.682, f32[16,256,6]{1,2,0:T(8,128)S(1)} %get-tuple-element.1053, f32[16,6,256]{2,1,0:T(8,128)S(1)} %bitcast.705, f32[16,256,256]{2,1,0:T(8,128)S(1)} %copy-done.41, f32[16,6,256]{2,1,0:T(8,128)S(1)} %copy-done.75, pred[256,256]{1,0:T(8,128)(4,1)S(1)} %copy-done.80, ...), kind=kOutput, calls=%fused_computation.136 | convolution fusion | flops 4866441216 | bytes 23429120 | tf_op jit(solution)/shard_map/transpose(jvp(jvp()))/checkpoint/bhij,bjhp->bihp/dot_general | solution.py:52
  1108.8 20.0 %rev.37 = f32[4096,6,64]{0,2,1:T(8,128)} reverse(f32[4096,6,64]{0,2,1:T(8,128)} %bitcast.665), dimensions={0} | reverse | bytes 12582912 | tf_op jit(solution)/shard_map/transpose(jvp())/rev | solution.py:113
  1128.8 14.9 reduce-window.50
  1144.1 14.9 reduce-window.56
  1187.4 19.2 %multiply_reduce_fusion.23 = (f32[256]{0:T(256)}, f32[256]{0:T(256)}, f32[256]{0:T(256)}, f32[256]{0:T(256)}, f32[256]{0:T(256)}, /*index=5*/f32[256]{0:T(256)}, f32[256]{0:T(256)}, f32[4096,256]{1,0:T(8,128)S(1)}) fusion(f32[4096,256]{1,0:T(8,128)} %copy-done.13, pred[4096]{0:T(1024)(128)(4,1)S(1)} %copy-done.58, pred[4096]{0:T(1024)(128)(4,1)S(1)} %copy-done.64, ...), kind=kLoop, calls=%fused_computation.229 | loop fusion | flops 34601216 | bytes 16813056 | tf_op jit(solution)/shard_map/transpose(jvp())/reduce_sum | solution.py:34
  1226.7 13.5 add_add_fusion
  1240.2 16.0 multiply_reduce_fusion.13
  1256.3 16.6 multiply_select_fusion.8
  1272.9 20.8 %pad_add_fusion = f32[4096,384]{0,1:T(8,128)} fusion(f32[4096,384]{0,1:T(8,128)} %get-tuple-element.1031, f32[4096,384]{0,1:T(8,128)} %get-tuple-element.1032, f32[4096,384]{0,1:T(8,128)} %get-tuple-element.1033, f32[4096,384]{0,1:T(8,128)} %get-tuple-element.1034, f32[4096,384]{0,1:T(8,128)} %get-tuple-element.1035, f32[4096,384]{0,1:T(8,128)} %get-tuple-element.1036, ...), kind=kLoop, calls=%fused_computation.121 | loop fusion | flops 9437184 | bytes 50331648 | tf_op jit(solution)/shard_map/transpose(jvp())/add_any | solution.py:32
  1365.8 152.4 %all-reduce.55 = (bf16[6,768,194]{1,2,0:T(8,128)(2,1)S(1)}, f32[6,10,64]{2,0,1:T(8,128)}) all-reduce(f32[6,768,194]{1,2,0:T(8,128)} %pad_maximum_fusion, f32[6,10,64]{2,0,1:T(8,128)S(1)} %fusion.243), channel_id=1, replica_groups=mesh['dp'=8,'mp'=4] {'dp'}, use_global_device_ids=true, to_apply=%region_44.45 | all-reduce | flops 897792 | bytes 5394432 | tf_op jit(solution)/shard_map/psum | solution.py:248
  1518.2 27.8 %fusion.117 = f32[1,768,194]{0,1,2:T(8,128)} fusion(bf16[6,768,194]{1,2,0:T(8,128)(2,1)S(1)} %get-tuple-element.986, s32[]{:T(128)S(6)} %axis_index.25, s32[24]{0:T(128)S(1)} %copy-done.135, s32[]{:T(128)S(6)} %select_n.236), kind=kOutput, calls=%fused_computation.213 | convolution fusion | flops 1787910 | bytes 2383976 | tf_op jit(solution)/shard_map/dot_general | solution.py:256
  1546.0 44.1 %copy.735 = f32[1,768,194]{1,2,0:T(8,128)S(1)} copy(f32[1,768,194]{0,1,2:T(8,128)} %fusion.117) | data formatting | bytes 1191936 | tf_op jit(solution)/shard_map/dot_general | solution.py:256
  1607.1 38.6 %psum.47 = f32[10,256]{1,0:T(8,128)S(1)} all-reduce(f32[10,256]{1,0:T(8,128)S(1)} %pad_maximum_fusion.1), channel_id=1, replica_groups=mesh['dp'=8,'mp'=4] {'dp','mp'}, use_global_device_ids=true, to_apply=%region_65.66 | all-reduce | flops 2560 | bytes 20480 | tf_op jit(solution)/shard_map/psum | solution.py:249
  (1079 shorter events, 786.3 us)
Async XLA Ops:
  7.2 59.5 %all-gather.9.cloned.1.call-start = ((), (), s32[]{:S(2)}) async-start(), calls=%async_computation.9 | async-start | bytes 2764800 | tf_op jit(solution)/shard_map/all_gather | solution.py:160
  9.1 104.7 %all-gather.5.cloned.1.call-start = ((), (), s32[]{:S(2)}) async-start(), calls=%async_computation.3 | async-start | bytes 7864320 | tf_op jit(solution)/shard_map/all_gather | solution.py:171
  15.9 528.9 %all-gather.7.cloned.1.call-start = ((), (), s32[]{:S(2)}) async-start(), calls=%async_computation.5 | async-start | bytes 7864320 | tf_op jit(solution)/shard_map/all_gather | solution.py:198
  16.6 1286.3 %reduce-scatter.8.cloned.1.call-start = ((), (), s32[]{:S(2)}) async-start(), calls=%async_computation.7 | async-start | bytes 5242880 | tf_op jit(solution)/shard_map/reduce_scatter | solution.py:216
  17.6 100.9 %copy-start.118 = (f32[1,256]{1,0:T(1,128)}, f32[1,256]{1,0:T(1,128)S(1)}, u32[]{:S(2)}) copy-start(f32[1,256]{1,0:T(1,128)S(1)} %get-tuple-element.1077) | copy-start | bytes 3076
  17.6 100.9 %copy-start.120 = (f32[1,256]{1,0:T(1,128)}, f32[1,256]{1,0:T(1,128)S(1)}, u32[]{:S(2)}) copy-start(f32[1,256]{1,0:T(1,128)S(1)} %get-tuple-element.1078) | copy-start | bytes 3076
  17.6 100.9 %copy-start.122 = (f32[1,256]{1,0:T(1,128)}, f32[1,256]{1,0:T(1,128)S(1)}, u32[]{:S(2)}) copy-start(f32[1,256]{1,0:T(1,128)S(1)} %get-tuple-element.1079) | copy-start | bytes 3076
  17.7 100.9 %copy-start.124 = (f32[1,256]{1,0:T(1,128)}, f32[1,256]{1,0:T(1,128)S(1)}, u32[]{:S(2)}) copy-start(f32[1,256]{1,0:T(1,128)S(1)} %get-tuple-element.1080) | copy-start | bytes 3076
  17.7 100.9 %copy-start.126 = (f32[1,256]{1,0:T(1,128)}, f32[1,256]{1,0:T(1,128)S(1)}, u32[]{:S(2)}) copy-start(f32[1,256]{1,0:T(1,128)S(1)} %get-tuple-element.1081) | copy-start | bytes 3076
  17.7 100.9 %copy-start.128 = (f32[1,256]{1,0:T(1,128)}, f32[1,256]{1,0:T(1,128)S(1)}, u32[]{:S(2)}) copy-start(f32[1,256]{1,0:T(1,128)S(1)} %get-tuple-element.1082) | copy-start | bytes 3076
  17.7 100.9 %copy-start.130 = (f32[1,256]{1,0:T(1,128)}, f32[1,256]{1,0:T(1,128)S(1)}, u32[]{:S(2)}) copy-start(f32[1,256]{1,0:T(1,128)S(1)} %get-tuple-element.1083) | copy-start | bytes 3076
  17.7 139.2 %copy-start.90 = (f32[6,2]{1,0:T(8,128)}, f32[6,2]{1,0:T(8,128)S(1)}, u32[]{:S(2)}) copy-start(f32[6,2]{1,0:T(8,128)S(1)} %slice_bitcast_fusion.4) | copy-start | bytes 148
  17.7 507.8 %copy-start.94 = (f32[6,64]{1,0:T(8,128)}, f32[6,64]{1,0:T(8,128)S(1)}, u32[]{:S(2)}) copy-start(f32[6,64]{1,0:T(8,128)S(1)} %get-tuple-element.1067) | copy-start | bytes 4612
  17.7 545.0 %copy-start.92 = (f32[6,64]{1,0:T(8,128)}, f32[6,64]{1,0:T(8,128)S(1)}, u32[]{:S(2)}) copy-start(f32[6,64]{1,0:T(8,128)S(1)} %get-tuple-element.1066) | copy-start | bytes 4612
  19.5 153.6 %copy-start.53 = (pred[4096]{0:T(1024)(128)(4,1)}, pred[4096]{0:T(1024)(128)(4,1)S(1)}, u32[]{:S(2)}) copy-start(pred[4096]{0:T(1024)(128)(4,1)S(1)} %get-tuple-element.1095) | copy-start | bytes 12292
  19.5 153.6 %copy-start.55 = (pred[4096]{0:T(1024)(128)(4,1)}, pred[4096]{0:T(1024)(128)(4,1)S(1)}, u32[]{:S(2)}) copy-start(pred[4096]{0:T(1024)(128)(4,1)S(1)} %get-tuple-element.1096) | copy-start | bytes 12292
  19.7 153.4 %copy-start.57 = (pred[4096]{0:T(1024)(128)(4,1)}, pred[4096]{0:T(1024)(128)(4,1)S(1)}, u32[]{:S(2)}) copy-start(pred[4096]{0:T(1024)(128)(4,1)S(1)} %get-tuple-element.1093) | copy-start | bytes 12292
  19.8 153.4 %copy-start.59 = (pred[4096]{0:T(1024)(128)(4,1)}, pred[4096]{0:T(1024)(128)(4,1)S(1)}, u32[]{:S(2)}) copy-start(pred[4096]{0:T(1024)(128)(4,1)S(1)} %get-tuple-element.1094) | copy-start | bytes 12292
  20.0 153.2 %copy-start.61 = (pred[4096]{0:T(1024)(128)(4,1)}, pred[4096]{0:T(1024)(128)(4,1)S(1)}, u32[]{:S(2)}) copy-start(pred[4096]{0:T(1024)(128)(4,1)S(1)} %get-tuple-element.1097) | copy-start | bytes 12292
  20.0 153.2 %copy-start.63 = (pred[4096]{0:T(1024)(128)(4,1)}, pred[4096]{0:T(1024)(128)(4,1)S(1)}, u32[]{:S(2)}) copy-start(pred[4096]{0:T(1024)(128)(4,1)S(1)} %get-tuple-element.1098) | copy-start | bytes 12292
  20.2 153.0 %copy-start.65 = (pred[4096]{0:T(1024)(128)(4,1)}, pred[4096]{0:T(1024)(128)(4,1)S(1)}, u32[]{:S(2)}) copy-start(pred[4096]{0:T(1024)(128)(4,1)S(1)} %get-tuple-element.1100) | copy-start | bytes 12292
  21.0 152.2 %copy-start.96 = (f32[384]{0:T(512)}, f32[384]{0:T(512)S(1)}, u32[]{:S(2)}) copy-start(f32[384]{0:T(512)S(1)} %mul.978) | copy-start | bytes 4612
  21.0 152.1 %copy-start.98 = (f32[384]{0:T(512)}, f32[384]{0:T(512)S(1)}, u32[]{:S(2)}) copy-start(f32[384]{0:T(512)S(1)} %mul.996) | copy-start | bytes 4612
  21.1 152.1 %copy-start.100 = (f32[384]{0:T(512)}, f32[384]{0:T(512)S(1)}, u32[]{:S(2)}) copy-start(f32[384]{0:T(512)S(1)} %mul.993) | copy-start | bytes 4612
  21.2 152.0 %copy-start.102 = (f32[384]{0:T(512)}, f32[384]{0:T(512)S(1)}, u32[]{:S(2)}) copy-start(f32[384]{0:T(512)S(1)} %mul.990) | copy-start | bytes 4612
  21.3 151.9 %copy-start.104 = (f32[384]{0:T(512)}, f32[384]{0:T(512)S(1)}, u32[]{:S(2)}) copy-start(f32[384]{0:T(512)S(1)} %mul.987) | copy-start | bytes 4612
  21.4 151.9 %copy-start.106 = (f32[384]{0:T(512)}, f32[384]{0:T(512)S(1)}, u32[]{:S(2)}) copy-start(f32[384]{0:T(512)S(1)} %mul.984) | copy-start | bytes 4612
  21.4 151.8 %copy-start.108 = (f32[384]{0:T(512)}, f32[384]{0:T(512)S(1)}, u32[]{:S(2)}) copy-start(f32[384]{0:T(512)S(1)} %mul.981) | copy-start | bytes 4612
  855.1 147.1 %copy-start.46 = (f32[16,6,256]{2,0,1:T(8,128)}, f32[16,6,256]{2,0,1:T(8,128)S(1)}, u32[]{:S(2)}) copy-start(f32[16,6,256]{2,0,1:T(8,128)S(1)} %copy_bitcast_fusion.4) | copy-start | bytes 294916
  1219.5 378.4 %all-reduce.54.cloned.1.call-start = ((), (), s32[]{:S(2)}) async-start(), calls=%async_computation.8 | async-start | bytes 1572864 | tf_op jit(solution)/shard_map/psum | solution.py:249
  1305.6 296.4 %reduce-scatter.6.cloned.1.call-start = ((), (), s32[]{:S(2)}) async-start(), calls=%async_computation.6 | async-start | bytes 15728640 | tf_op jit(solution)/shard_map/reduce_scatter | solution.py:230
  1318.1 328.3 %reduce-scatter.4.cloned.1.call-start = ((), (), s32[]{:S(2)}) async-start(), calls=%async_computation.4 | async-start | bytes 15728640 | tf_op jit(solution)/shard_map/reduce_scatter | solution.py:191
  (145 other events, 2384.6 us)
Sparse Core Ops, SparseCore 0:
  10.8 55.9 all-gather.8
  68.9 44.9 all-gather.4
  115.4 46.3 all-gather.6
  1219.6 45.7 reduce-scatter.7
  1305.8 135.6 all-reduce.53
  1443.9 97.4 reduce-scatter.5
  1544.0 99.9 reduce-scatter.3
where the time goes:
time: 1680 us; the launch traced here: 1660 us
  local copies, waits for them, and re-layouts  457 us (27%)
  matrix products  457 us (27%)
  other arithmetic  428 us (25%)
  blocking collectives  211 us (13%)
  waiting for transfers between devices  85.3 us (5%)
  between operations  18.2 us (1%)
    dot_general x6, matrix products, within_blocks(): jnp.einsum('bhij,bjhp->bihp', weights, values_blk, precision=PRECISE)  219 us
    psum x1, blocking collectives, local(): block_total, params_total = lax.psum((block_grad, params_grad), 'dp')  152 us
    dynamic_slice x192, local copies, waits for them, and re-layouts, state_mix(): lax.scan(carry_state, initial, (local_state, log_decay[:, :, -1], keep_fl...  105 us
    dynamic_update_slice x64, other arithmetic, state_mix(): lax.scan(carry_state, initial, (local_state, log_decay[:, :, -1], keep_fl...  65.3 us
    dot_general x6, matrix products, within_blocks(): jnp.einsum('bjn,bhj,bjhp->bhnp', b_blk, tail_decay, values_blk, precision...  61.2 us
    reduce_sum x32, other arithmetic, carry_state(): new_state = entering * jnp.exp(total_decay)[:, None, None] + local_state  54.8 us
    unnamed x347, local copies, waits for them, and re-layouts  52.1 us
    dot_general x8, matrix products, within_blocks(): scores = jnp.einsum('bin,bjn->bij', c_blk, b_blk, precision=PRECISE)  47.9 us
  transfers between devices with their start and end apart: 7, of which 2 were waited for; matrix products, arithmetic and copies ran while one was open for 40% of the time, Pallas kernels for 0%

commit v1 on v0

--- a/solution.py
+++ b/solution.py
@@ -18,6 +18,7 @@
 MATRIX_RATE = 0.04
 SMALL_RATE = 0.2
 AVERAGE_KEEP = 0.75
+_replace_waves = lambda mat: jax.lax.psum(jax.lax.psum(mat, "mp"), "dp")
 
 
 def conv_centered(signal, filter_taps, seq_length):
@@ -246,7 +247,7 @@
     )
     shared_grad = jnp.concatenate([taps_grad, gain_in_grad.reshape(-1, taps_grad.shape[1])], axis=0)
     block_total, params_total = lax.psum((block_grad, params_grad), "dp")
-    key_total, shared_total = lax.psum((key_weight_grad, shared_grad), ("dp", "mp"))
+    key_total, shared_total = _replace_waves((key_weight_grad, shared_grad))
     head_new = adamw_update(head_small, params_total, head_first, head_second, head_ema, SMALL_RATE)
     key_new = adamw_update(bc_weight, key_total, bc_first, bc_second, bc_ema, MATRIX_RATE)
     shared_new = adamw_update(

time: 1680 us -> 1790 us (1.065)
  waiting for transfers between devices: 85.3 us -> 228 us
  blocking collectives: 211 us -> 183 us
    reduce_scatter x1, waiting for transfers between devices: 0.02 us -> 96.8 us  [local(): lax.psum_scatter(lax.dot_general(rows_in, w_in_flat, (((1,), (1,)), ((),...]
    psum x1 -> x2, waiting for transfers between devices: 0.01 us -> 45.9 us  [_replace_waves = lambda mat: jax.lax.psum(jax.lax.psum(mat, 'mp'), 'dp')]
    psum x1, blocking collectives: 38.6 us -> 10.1 us  [_replace_waves = lambda mat: jax.lax.psum(jax.lax.psum(mat, 'mp'), 'dp')]
    unnamed x347 -> x349, local copies, waits for them, and re-layouts: 52.1 us -> 52.1 us
  transfers between devices with their start and end apart: 7 -> 8, of which waited for: 2 -> 5; matrix products, arithmetic and copies ran while one was open for 40% -> 38% of each run, Pallas kernels for 0% -> 0%
where the time goes in v1:
time: 1790 us; the launch traced here: 1770 us
  matrix products  457 us (26%)
  local copies, waits for them, and re-layouts  453 us (25%)
  other arithmetic  428 us (24%)
  waiting for transfers between devices  228 us (13%)
  blocking collectives  183 us (10%)
  between operations  18.5 us (1%)
    dot_general x6, matrix products, within_blocks(): jnp.einsum('bhij,bjhp->bihp', weights, values_blk, precision=PRECISE)  219 us
    psum x1, blocking collectives, local(): block_total, params_total = lax.psum((block_grad, params_grad), 'dp')  152 us
    dynamic_slice x192, local copies, waits for them, and re-layouts, state_mix(): lax.scan(carry_state, initial, (local_state, log_decay[:, :, -1], keep_fl...  105 us
    reduce_scatter x1, waiting for transfers between devices, local(): lax.psum_scatter(lax.dot_general(rows_in, w_in_flat, (((1,), (1,)), ((),...  96.8 us
    dynamic_update_slice x64, other arithmetic, state_mix(): lax.scan(carry_state, initial, (local_state, log_decay[:, :, -1], keep_fl...  65.5 us
    dot_general x6, matrix products, within_blocks(): jnp.einsum('bjn,bhj,bjhp->bhnp', b_blk, tail_decay, values_blk, precision...  61.1 us
    reduce_sum x32, other arithmetic, carry_state(): new_state = entering * jnp.exp(total_decay)[:, None, None] + local_state  54.8 us
    unnamed x349, local copies, waits for them, and re-layouts  52.1 us
  transfers between devices with their start and end apart: 8, of which 5 were waited for; matrix products, arithmetic and copies ran while one was open for 38% of the time, Pallas kernels for 0%

profile of v1, /device:TPU:0, one launch (start us, length us, event | category | flops | bytes accessed | tf_op | source)
XLA Modules:
  0.0 1770.0 jit_solution(13269272587551942200)
XLA Ops:
  21.4 45.3 %all-gather.9.cloned.1.call-done = bf16[8,1,768,194]{2,3,1,0:T(8,128)(2,1)} async-done(((bf16[1,1,768,194]{2,3,1,0:T(8,128)(2,1)}), bf16[8,1,768,194]{2,3,1,0:T(8,128)(2,1)}) %all-gather.9.cloned.1.call-update) | async-done | bytes 2383888 | tf_op jit(solution)/shard_map/all_gather | solution.py:161
  74.7 39.1 %all-gather.5.cloned.1.call-done = bf16[4096,768]{1,0:T(8,128)(2,1)} async-done(((bf16[1024,768]{1,0:T(8,128)(2,1)}), bf16[4096,768]{1,0:T(8,128)(2,1)}) %all-gather.5.cloned.1.call-update) | async-done | bytes 6291472 | tf_op jit(solution)/shard_map/all_gather | solution.py:172
  132.0 13.7 rev.33
  173.2 28.8 %fusion.98 = (f32[4096,384]{0,1:T(8,128)}, f32[4096,384]{0,1:T(8,128)}) fusion(f32[384]{0:T(512)S(1)} %mul.996, pred[4096]{0:T(1024)(128)(4,1)S(1)} %get-tuple-element.1094, f32[384]{0:T(512)S(1)} %mul.993, pred[4096]{0:T(1024)(128)(4,1)S(1)} %get-tuple-element.1095, f32[384]{0:T(512)S(1)} %mul.990, pred[4096]{0:T(1024)(128)(4,1)S(1)} %get-tuple-element.1096, ...), kind=kLoop, calls=%fused_computation.187 | loop fusion | flops 37748736 | bytes 18913792 | tf_op jit(solution)/shard_map/jvp(jit(silu))/mul | solution.py:98
  202.0 20.0 %rev.30 = f32[4096,6,64]{0,2,1:T(8,128)} reverse(f32[4096,6,64]{0,2,1:T(8,128)} %bitcast.605), dimensions={0} | reverse | bytes 12582912 | tf_op jit(solution)/shard_map/jvp()/rev | solution.py:114
  233.1 60.8 %while.74 = (s32[]{:T(128)}, f32[6,64,64]{2,1,0:T(8,128)S(1)}, f32[16,6,64,64]{3,2,1,0:T(8,128)}, f32[16,6]{1,0:T(8,128)S(1)}, f32[16,6,1,1]{1,3,2,0:T(1,128)S(1...) while((s32[]{:T(128)}, f32[6,64,64]{2,1,0:T(8,128)S(1)}, ...), condition=%wide.region_8.9_spmd.clone, body=%wide.region_7.8_spmd.clone.sunk | while | flops 147459 | bytes 985312 | solution.py:80
  316.1 60.6 %while.73 = (s32[]{:T(128)}, f32[6,64,64]{2,1,0:T(8,128)S(1)}, f32[16,6,64,64]{3,2,1,0:T(8,128)}, f32[16,6]{1,0:T(8,128)S(1)}, f32[16,6,1,1]{1,3,2,0:T(1,128)S(1...) while((s32[]{:T(128)}, f32[6,64,64]{2,1,0:T(8,128)S(1)}, ...), condition=%wide.region_4.5_spmd.clone, body=%wide.region_3.4_spmd.clone.sunk | while | flops 147459 | bytes 985312 | solution.py:80
  376.7 16.6 rev.32
  411.2 29.4 %fusion.84 = f32[16,6,8,8,256]{4,3,2,1,0:T(8,128)S(1)} fusion(f32[16,256,6,64]{1,3,2,0:T(8,128)S(1)} %bitcast.666, f32[16,256,6]{1,2,0:T(8,128)S(1)} %get-tuple-element.1066, f32[16,6,256]{2,1,0:T(8,128)S(1)} %copy.611, f32[16,256,256]{2,1,0:T(8,128)S(1)} %fusion.278, f32[16,6,256]{2,1,0:T(8,128)S(1)} %get-tuple-element.1065, ...), kind=kOutput, calls=%fused_computation.144 | convolution fusion | flops 4866441216 | bytes 23429120 | tf_op jit(solution)/shard_map/jvp(bhij,bjhp->bihp)/dot_general | solution.py:53
  445.7 20.0 %rev.34 = f32[4096,6,64]{0,2,1:T(8,128)} reverse(f32[4096,6,64]{0,2,1:T(8,128)} %pad_select_fusion), dimensions={0} | reverse | bytes 12582912 | tf_op jit(solution)/shard_map/jvp()/rev | solution.py:112
  484.5 34.6 %fusion.85 = f32[16,6,8,8,256]{4,3,2,1,0:T(8,128)} fusion(f32[16,256,6,64]{1,3,2,0:T(8,128)} %bitcast.668, f32[16,256,6]{1,2,0:T(8,128)S(1)} %get-tuple-element.1064, f32[16,6,256]{2,1,0:T(8,128)S(1)} %copy.593, f32[16,256,256]{2,1,0:T(8,128)} %fusion.276, f32[16,6,256]{2,1,0:T(8,128)S(1)} %get-tuple-element.1063, pred[256,256]{1,0:T(8,128)(4,1)S(1)} %copy-done.80, ...), kind=kOutput, calls=%fused_computation.146 | convolution fusion | flops 4866441216 | bytes 23429120 | tf_op jit(solution)/shard_map/jvp(bhij,bjhp->bihp)/dot_general | solution.py:53
  562.7 17.4 multiply_reduce_fusion.14
  580.2 20.2 %rev.35 = f32[4096,6,64]{0,2,1:T(8,128)} reverse(f32[4096,6,64]{0,2,1:T(8,128)} %get-tuple-element.1009), dimensions={0} | reverse | bytes 12582912 | tf_op jit(solution)/shard_map/transpose(jvp())/rev | solution.py:112
  648.9 77.2 %while.76 = (s32[]{:T(128)}, f32[6,64,64]{2,1,0:T(8,128)S(1)}, f32[16,6,64,64]{3,2,1,0:T(8,128)}, f32[16,6]{1,0:T(8,128)S(1)}, f32[16,6,64,64]{2,3,1,0:T(8,128)}...) while((s32[]{:T(128)}, f32[6,64,64]{2,1,0:T(8,128)S(1)}, ...), condition=%wide.region_28.29_spmd.clone, body=%wide.region_26.28_spmd.clone.sunk | while | flops 172036 | bytes 1081748 | solution.py:80
  754.6 87.3 %while.75 = (s32[]{:T(128)}, f32[6,64,64]{2,1,0:T(8,128)S(1)}, f32[16,6,64,64]{3,2,1,0:T(8,128)}, f32[16,6]{1,0:T(8,128)S(1)}, f32[16,6,64,64]{2,3,1,0:T(8,128)}...) while((s32[]{:T(128)}, f32[6,64,64]{2,1,0:T(8,128)S(1)}, ...), condition=%wide.region_16.17_spmd.clone, body=%wide.region_14.16_spmd.clone.sunk | while | flops 172036 | bytes 1081748 | solution.py:80
  900.4 35.4 %fusion.79 = f32[16,6,256,256]{3,2,1,0:T(8,128)} fusion(f32[16,256,6,64]{1,0,3,2:T(8,128)} %bitcast.598, f32[16,256,6,64]{1,0,3,2:T(8,128)} %bitcast.655), kind=kOutput, calls=%fused_computation.138 | convolution fusion | flops 4831838208 | bytes 37748736 | tf_op jit(solution)/shard_map/transpose(jvp(jvp()))/checkpoint/bhij,bjhp->bihp/dot_general | solution.py:53
  935.9 66.3 %fusion.35 = (f32[16,6,256]{2,1,0:T(8,128)}, f32[16,6,256]{2,1,0:T(8,128)}, f32[16,6,256]{2,1,0:T(8,128)}, f32[16,256,256]{2,1,0:T(8,128)}, f32[16,256,256]{2,1,...) fusion(f32[16,6,256]{2,1,0:T(8,128)S(1)} %bitcast.704, ...), kind=kOutput, calls=%fused_computation.67 | convolution fusion | flops 5018337280 | bytes 55574528 | tf_op jit(solution)/shard_map/transpose(jvp(jvp()))/checkpoint/bhij,bjhp->bihp/dot_general | solution.py:53
  1012.5 27.1 %fusion.76 = f32[16,6,8,8,256]{4,3,2,1,0:T(8,128)} fusion(f32[16,256,6,64]{1,3,2,0:T(8,128)S(1)} %copy-done.38, f32[16,256,6]{1,2,0:T(8,128)S(1)} %get-tuple-element.1056, f32[16,6,256]{2,1,0:T(8,128)S(1)} %bitcast.703, f32[16,256,256]{2,1,0:T(8,128)} %fusion.282, f32[16,6,256]{2,1,0:T(8,128)S(1)} %copy-done.78, pred[256,256]{1,0:T(8,128)(4,1)S(1)} %copy-done.81, ...), kind=kOutput, calls=%fused_computation.134 | convolution fusion | flops 4866441216 | bytes 23429120 | tf_op jit(solution)/shard_map/transpose(jvp(jvp()))/checkpoint/bhij,bjhp->bihp/dot_general | solution.py:53
  1068.7 26.4 %fusion.77 = f32[16,6,8,8,256]{4,3,2,1,0:T(8,128)} fusion(f32[16,256,6,64]{1,3,2,0:T(8,128)S(1)} %bitcast.682, f32[16,256,6]{1,2,0:T(8,128)S(1)} %get-tuple-element.1054, f32[16,6,256]{2,1,0:T(8,128)S(1)} %bitcast.705, f32[16,256,256]{2,1,0:T(8,128)S(1)} %copy-done.42, f32[16,6,256]{2,1,0:T(8,128)S(1)} %copy-done.77, pred[256,256]{1,0:T(8,128)(4,1)S(1)} %copy-done.81, ...), kind=kOutput, calls=%fused_computation.136 | convolution fusion | flops 4866441216 | bytes 23429120 | tf_op jit(solution)/shard_map/transpose(jvp(jvp()))/checkpoint/bhij,bjhp->bihp/dot_general | solution.py:53
  1110.5 20.0 %rev.37 = f32[4096,6,64]{0,2,1:T(8,128)} reverse(f32[4096,6,64]{0,2,1:T(8,128)} %bitcast.665), dimensions={0} | reverse | bytes 12582912 | tf_op jit(solution)/shard_map/transpose(jvp())/rev | solution.py:114
  1130.5 14.9 reduce-window.50
  1173.5 19.2 %multiply_reduce_fusion.23 = (f32[256]{0:T(256)}, f32[256]{0:T(256)}, f32[256]{0:T(256)}, f32[256]{0:T(256)}, f32[256]{0:T(256)}, /*index=5*/f32[256]{0:T(256)}, f32[256]{0:T(256)}, f32[4096,256]{1,0:T(8,128)S(1)}) fusion(f32[4096,256]{1,0:T(8,128)} %copy-done.13, pred[4096]{0:T(1024)(128)(4,1)S(1)} %copy-done.60, pred[4096]{0:T(1024)(128)(4,1)S(1)} %copy-done.66, ...), kind=kLoop, calls=%fused_computation.229 | loop fusion | flops 34601216 | bytes 16813056 | tf_op jit(solution)/shard_map/transpose(jvp())/reduce_sum | solution.py:35
  1206.4 14.9 reduce-window.56
  1240.8 16.0 multiply_reduce_fusion.13
  1256.9 16.7 multiply_select_fusion.8
  1273.6 21.3 %pad_add_fusion = f32[4096,384]{0,1:T(8,128)} fusion(f32[4096,384]{0,1:T(8,128)} %get-tuple-element.1032, f32[4096,384]{0,1:T(8,128)} %get-tuple-element.1033, f32[4096,384]{0,1:T(8,128)} %get-tuple-element.1034, f32[4096,384]{0,1:T(8,128)} %get-tuple-element.1035, f32[4096,384]{0,1:T(8,128)} %get-tuple-element.1036, f32[4096,384]{0,1:T(8,128)} %get-tuple-element.1037, ...), kind=kLoop, calls=%fused_computation.121 | loop fusion | flops 9437184 | bytes 50331648 | tf_op jit(solution)/shard_map/transpose(jvp())/add_any | solution.py:33
  1306.1 27.6 %all-reduce.55.cloned.1.call-done = f32[768,256]{1,0:T(8,128)} async-done(((f32[768,256]{1,0:T(8,128)}), f32[768,256]{1,0:T(8,128)}) %all-reduce.55.cloned.1.call-update) | async-done | bytes 786448 | tf_op jit(solution)/shard_map/psum | solution.py:21
  1393.9 18.3 %all-reduce.57.cloned.1.call-done = f32[768,256]{1,0:T(8,128)} async-done(((f32[768,256]{1,0:T(8,128)}), f32[768,256]{1,0:T(8,128)}) %all-reduce.57.cloned.1.call-update) | async-done | bytes 786448 | tf_op jit(solution)/shard_map/psum | solution.py:21
  1416.2 96.8 %reduce-scatter.6.cloned.1.call-done = f32[1024,768]{1,0:T(8,128)} async-done(((f32[4096,768]{1,0:T(8,128)}), f32[1024,768]{1,0:T(8,128)}) %reduce-scatter.6.cloned.1.call-update) | async-done | bytes 3145744 | tf_op jit(solution)/shard_map/reduce_scatter | solution.py:231
  1527.9 152.5 %all-reduce.58 = (bf16[6,768,194]{1,2,0:T(8,128)(2,1)S(1)}, f32[6,10,64]{2,0,1:T(8,128)S(1)}, f32[10,256]{1,0:T(8,128)S(1)}) all-reduce(f32[6,768,194]{1,2,0:T(8,128)} %pad_maximum_fusion, f32[6,10,64]{2,0,1:T(8,128)S(1)} %fusion.243, f32[10,256]{1,0:T(8,128)S(1)} %psum.62), channel_id=1, replica_groups=mesh['dp'=8,'mp'=4] {'dp'}, use_global_device_ids=true, to_apply=%region_44.45 | all-reduce | flops 900352 | bytes 5414912 | tf_op jit(solution)/shard_map/psum | solution.py:249
  1680.3 27.5 %fusion.117 = f32[1,768,194]{0,1,2:T(8,128)} fusion(bf16[6,768,194]{1,2,0:T(8,128)(2,1)S(1)} %get-tuple-element.986, s32[]{:T(128)S(6)} %axis_index.25, s32[24]{0:T(128)S(1)} %copy-done.136, s32[]{:T(128)S(6)} %select_n.236), kind=kOutput, calls=%fused_computation.213 | convolution fusion | flops 1787910 | bytes 2383976 | tf_op jit(solution)/shard_map/dot_general | solution.py:257
  1707.9 40.9 %copy.735 = f32[1,768,194]{1,2,0:T(8,128)} copy(f32[1,768,194]{0,1,2:T(8,128)} %fusion.117) | data formatting | bytes 1191936 | tf_op jit(solution)/shard_map/dot_general | solution.py:257
  (1084 shorter events, 821.7 us)
Async XLA Ops:
  7.2 59.5 %all-gather.9.cloned.1.call-start = ((), (), s32[]{:S(2)}) async-start(), calls=%async_computation.10 | async-start | bytes 2764800 | tf_op jit(solution)/shard_map/all_gather | solution.py:161
  9.1 104.7 %all-gather.5.cloned.1.call-start = ((), (), s32[]{:S(2)}) async-start(), calls=%async_computation.3 | async-start | bytes 7864320 | tf_op jit(solution)/shard_map/all_gather | solution.py:172
  15.9 528.9 %all-gather.7.cloned.1.call-start = ((), (), s32[]{:S(2)}) async-start(), calls=%async_computation.5 | async-start | bytes 7864320 | tf_op jit(solution)/shard_map/all_gather | solution.py:199
  16.6 1278.3 %reduce-scatter.8.cloned.1.call-start = ((), (), s32[]{:S(2)}) async-start(), calls=%async_computation.7 | async-start | bytes 5242880 | tf_op jit(solution)/shard_map/reduce_scatter | solution.py:217
  17.6 100.9 %copy-start.119 = (f32[1,256]{1,0:T(1,128)}, f32[1,256]{1,0:T(1,128)S(1)}, u32[]{:S(2)}) copy-start(f32[1,256]{1,0:T(1,128)S(1)} %get-tuple-element.1078) | copy-start | bytes 3076
  17.6 100.9 %copy-start.121 = (f32[1,256]{1,0:T(1,128)}, f32[1,256]{1,0:T(1,128)S(1)}, u32[]{:S(2)}) copy-start(f32[1,256]{1,0:T(1,128)S(1)} %get-tuple-element.1079) | copy-start | bytes 3076
  17.7 139.2 %copy-start.90 = (f32[6,2]{1,0:T(8,128)}, f32[6,2]{1,0:T(8,128)S(1)}, u32[]{:S(2)}) copy-start(f32[6,2]{1,0:T(8,128)S(1)} %slice_bitcast_fusion.4) | copy-start | bytes 148
  17.7 507.8 %copy-start.94 = (f32[6,64]{1,0:T(8,128)}, f32[6,64]{1,0:T(8,128)S(1)}, u32[]{:S(2)}) copy-start(f32[6,64]{1,0:T(8,128)S(1)} %get-tuple-element.1068) | copy-start | bytes 4612
  17.7 545.0 %copy-start.92 = (f32[6,64]{1,0:T(8,128)}, f32[6,64]{1,0:T(8,128)S(1)}, u32[]{:S(2)}) copy-start(f32[6,64]{1,0:T(8,128)S(1)} %get-tuple-element.1067) | copy-start | bytes 4612
  19.5 153.6 %copy-start.55 = (pred[4096]{0:T(1024)(128)(4,1)}, pred[4096]{0:T(1024)(128)(4,1)S(1)}, u32[]{:S(2)}) copy-start(pred[4096]{0:T(1024)(128)(4,1)S(1)} %get-tuple-element.1096) | copy-start | bytes 12292
  19.5 153.6 %copy-start.57 = (pred[4096]{0:T(1024)(128)(4,1)}, pred[4096]{0:T(1024)(128)(4,1)S(1)}, u32[]{:S(2)}) copy-start(pred[4096]{0:T(1024)(128)(4,1)S(1)} %get-tuple-element.1097) | copy-start | bytes 12292
  19.7 153.4 %copy-start.59 = (pred[4096]{0:T(1024)(128)(4,1)}, pred[4096]{0:T(1024)(128)(4,1)S(1)}, u32[]{:S(2)}) copy-start(pred[4096]{0:T(1024)(128)(4,1)S(1)} %get-tuple-element.1094) | copy-start | bytes 12292
  19.8 153.4 %copy-start.61 = (pred[4096]{0:T(1024)(128)(4,1)}, pred[4096]{0:T(1024)(128)(4,1)S(1)}, u32[]{:S(2)}) copy-start(pred[4096]{0:T(1024)(128)(4,1)S(1)} %get-tuple-element.1095) | copy-start | bytes 12292
  20.0 153.1 %copy-start.63 = (pred[4096]{0:T(1024)(128)(4,1)}, pred[4096]{0:T(1024)(128)(4,1)S(1)}, u32[]{:S(2)}) copy-start(pred[4096]{0:T(1024)(128)(4,1)S(1)} %get-tuple-element.1098) | copy-start | bytes 12292
  20.0 153.1 %copy-start.65 = (pred[4096]{0:T(1024)(128)(4,1)}, pred[4096]{0:T(1024)(128)(4,1)S(1)}, u32[]{:S(2)}) copy-start(pred[4096]{0:T(1024)(128)(4,1)S(1)} %get-tuple-element.1099) | copy-start | bytes 12292
  20.2 152.9 %copy-start.67 = (pred[4096]{0:T(1024)(128)(4,1)}, pred[4096]{0:T(1024)(128)(4,1)S(1)}, u32[]{:S(2)}) copy-start(pred[4096]{0:T(1024)(128)(4,1)S(1)} %get-tuple-element.1101) | copy-start | bytes 12292
  21.0 152.2 %copy-start.97 = (f32[384]{0:T(512)}, f32[384]{0:T(512)S(1)}, u32[]{:S(2)}) copy-start(f32[384]{0:T(512)S(1)} %mul.978) | copy-start | bytes 4612
  21.0 152.1 %copy-start.99 = (f32[384]{0:T(512)}, f32[384]{0:T(512)S(1)}, u32[]{:S(2)}) copy-start(f32[384]{0:T(512)S(1)} %mul.996) | copy-start | bytes 4612
  21.1 152.1 %copy-start.101 = (f32[384]{0:T(512)}, f32[384]{0:T(512)S(1)}, u32[]{:S(2)}) copy-start(f32[384]{0:T(512)S(1)} %mul.993) | copy-start | bytes 4612
  21.2 152.0 %copy-start.103 = (f32[384]{0:T(512)}, f32[384]{0:T(512)S(1)}, u32[]{:S(2)}) copy-start(f32[384]{0:T(512)S(1)} %mul.990) | copy-start | bytes 4612
  21.3 151.9 %copy-start.105 = (f32[384]{0:T(512)}, f32[384]{0:T(512)S(1)}, u32[]{:S(2)}) copy-start(f32[384]{0:T(512)S(1)} %mul.987) | copy-start | bytes 4612
  21.3 151.9 %copy-start.107 = (f32[384]{0:T(512)}, f32[384]{0:T(512)S(1)}, u32[]{:S(2)}) copy-start(f32[384]{0:T(512)S(1)} %mul.984) | copy-start | bytes 4612
  21.4 151.8 %copy-start.109 = (f32[384]{0:T(512)}, f32[384]{0:T(512)S(1)}, u32[]{:S(2)}) copy-start(f32[384]{0:T(512)S(1)} %mul.981) | copy-start | bytes 4612
  859.2 198.5 %copy-start.47 = (f32[16,6,256]{2,0,1:T(8,128)}, f32[16,6,256]{2,0,1:T(8,128)S(1)}, u32[]{:S(2)}) copy-start(f32[16,6,256]{2,0,1:T(8,128)S(1)} %copy_bitcast_fusion.5) | copy-start | bytes 294916
  1206.1 127.6 %all-reduce.55.cloned.1.call-start = ((), (), s32[]{:S(2)}) async-start(), calls=%async_computation.8 | async-start | bytes 1572864 | tf_op jit(solution)/shard_map/psum | solution.py:21
  1297.6 114.6 %all-reduce.57.cloned.1.call-start = ((), (), s32[]{:S(2)}) async-start(), calls=%async_computation.9 | async-start | bytes 1572864 | tf_op jit(solution)/shard_map/psum | solution.py:21
  1333.7 179.3 %reduce-scatter.6.cloned.1.call-start = ((), (), s32[]{:S(2)}) async-start(), calls=%async_computation.6 | async-start | bytes 15728640 | tf_op jit(solution)/shard_map/reduce_scatter | solution.py:231
  1346.1 411.6 %reduce-scatter.4.cloned.1.call-start = ((), (), s32[]{:S(2)}) async-start(), calls=%async_computation.4 | async-start | bytes 15728640 | tf_op jit(solution)/shard_map/reduce_scatter | solution.py:192
  1391.6 121.5 %copy-start.25 = (bf16[1024,768]{1,0:T(8,128)(2,1)S(1)}, bf16[1024,768]{1,0:T(8,128)(2,1)}, u32[]{:S(2)}) copy-start(bf16[1024,768]{1,0:T(8,128)(2,1)} %param.30) | copy-start | bytes 4718596
  1391.6 121.4 %copy-start.49 = (f32[1024,256]{1,0:T(8,128)S(1)}, f32[1024,256]{1,0:T(8,128)}, u32[]{:S(2)}) copy-start(f32[1024,256]{1,0:T(8,128)} %reduce-scatter.8.cloned.1.call-done) | copy-start | bytes 3145732
  1391.6 121.4 %copy-start.83 = (f32[1024]{0:T(1024)S(1)}, f32[1024]{0:T(1024)}, u32[]{:S(2)}) copy-start(f32[1024]{0:T(1024)} %copy-done.82) | copy-start | bytes 12292
  1391.6 121.4 %copy-start.85 = (f32[768]{0:T(1024)S(1)}, f32[768]{0:T(1024)}, u32[]{:S(2)}) copy-start(f32[768]{0:T(1024)} %copy-done.84) | copy-start | bytes 9220
  (147 other events, 2534.7 us)
Sparse Core Ops, SparseCore 0:
  10.8 55.9 all-gather.8
  68.9 44.9 all-gather.4
  115.4 46.3 all-gather.6
  1206.2 45.8 reduce-scatter.7
  1297.7 35.9 all-reduce.54
  1337.4 74.8 all-reduce.56
  1414.8 98.1 reduce-scatter.5
  1515.6 99.0 reduce-scatter.3
